TPU v7x, 32 devices: a whole 2x2x4 slice. The times are simulated.
32 devices in a mesh: row: 8 (over z, y), col: 4 (over x, core).
Axes of the slice: x: 2, y: 2, z: 4, core: 2. Of those that a mesh axis runs over, the one named last changes fastest.
Arguments:
- momentum: float32 [8192, 8192], P('row', 'col'), may hold values from -6 to 6
- gradient: bfloat16 [8192, 8192], P('row', 'col'), may hold values from -6 to 6
- weight: bfloat16 [8192, 8192], P('row', 'col'), may hold values from -6 to 6
- right_start: float32 [8192, 512], P('col', 'row'), may hold values from -0.0625 to 0.0625
Outputs:
- new_momentum: float32 [8192, 8192], P('row', 'col')
- new_weight: bfloat16 [8192, 8192], P('row', 'col')
- new_right: float32 [8192, 512], P('col', 'row')
All inputs are finite; a program needn't handle non-finite values.
Results may differ from a plain program's by a relative error of at most 0.001.
Values sent between devices are 32-bit elements; how exact they have to be, the bound alone decides.
A program may use at most 128 MiB of HBM per device.

v0:
```python
import jax
import jax.numpy as jnp
from jax import lax
from jax.sharding import PartitionSpec as P

ITERS = 2
BLOCK = 128
gram_mode = lax.Precision.HIGHEST
wide_mode = lax.Precision.HIGH
momentum_decay = 0.9
step_rate = 0.1
epsilon = 1e-06


def self_gram(rows):
    return lax.dot_general(rows, rows, (((0,), (0,)), ((), ())), precision=gram_mode)


def times_transposed(a, b):
    return lax.dot_general(a, b, (((1,), (1,)), ((), ())), precision=gram_mode)


def solve_rows(rows, gram_sum):
    rank = gram_sum.shape[0]
    block = min(BLOCK, rank)
    trailing = gram_sum
    rest = rows
    solved = []
    for at in range(0, rank, block):
        size = min(block, rank - at)
        corner = lax.linalg.cholesky(trailing[:size, :size], symmetrize_input=False)
        inverse = lax.linalg.triangular_solve(
            corner, jnp.eye(size, dtype=corner.dtype), left_side=True, lower=True
        )
        block_rows = times_transposed(rest[:, :size], inverse)
        solved.append(block_rows)
        if at + size < rank:
            panel = times_transposed(trailing[size:, :size], inverse)
            trailing = trailing[size:, size:] - times_transposed(panel, panel)
            rest = rest[:, size:] - times_transposed(block_rows, panel)
    return jnp.concatenate(solved, axis=1)


def shards(momentum, gradient, weight, right_start):
    rows_at, cols_at = (lax.psum(1, "row"), lax.psum(1, "col"))
    out_dim, in_dim = (momentum.shape[0] * rows_at, momentum.shape[1] * cols_at)
    rank = right_start.shape[1] * rows_at
    blended = momentum + gradient.astype(jnp.float32)
    right_full = lax.all_gather(right_start, "row", axis=1, tiled=True)
    right_shard = right_start
    for iteration in range(ITERS):
        partials = jnp.dot(blended, right_full, precision=wide_mode)
        left_sum = lax.psum(partials, "col")
        gram_sum = lax.psum(self_gram(left_sum), "row")
        left_rows = solve_rows(left_sum, gram_sum)
        transposed = lax.dot_general(
            blended, left_rows, (((0,), (0,)), ((), ())), precision=wide_mode
        )
        products = lax.psum_scatter(transposed, "row", scatter_dimension=1, tiled=True)
        squares = lax.psum(jnp.sum(products * products, axis=0, keepdims=True), "col")
        col_norms = jnp.sqrt(squares + epsilon)
        right_shard = products / col_norms
        products_full, norms_full = (
            lax.all_gather(products, "row", axis=1, tiled=True),
            lax.all_gather(col_norms, "row", axis=1, tiled=True),
        )
        right_full = products_full / norms_full
    outer_dims = (((1,), (1,)), ((), ()))
    feedback = lax.dot_general(left_rows, products_full, outer_dims, precision=wide_mode)
    new_momentum = blended - (1.0 - momentum_decay) * feedback
    scale_factor = step_rate * (out_dim * in_dim / rank) ** 0.5
    update = lax.dot_general(left_rows, right_full, outer_dims, precision=wide_mode)
    new_weight = (weight.astype(jnp.float32) - scale_factor * update).astype(jnp.bfloat16)
    return (new_momentum, new_weight, right_shard)


def solution(mesh):
    return jax.shard_map(
        shards,
        mesh=mesh,
        in_specs=(P("row", "col"), P("row", "col"), P("row", "col"), P("col", "row")),
        out_specs=(P("row", "col"), P("row", "col"), P("col", "row")),
        check_vma=False,
    )
```

profile of v0, /device:TPU:0, one launch (start us, length us, event | category | flops | bytes accessed | tf_op | source)
XLA Modules:
  0.0 969.1 jit_solution(15669869728964990464)
XLA Ops:
  7.9 77.7 %all-gather.4.cloned.1.call-done = f32[2048,512]{0,1:T(8,128)} async-done(((f32[2048,64]{0,1:T(8,128)}), f32[2048,512]{0,1:T(8,128)}) %all-gather.4.cloned.1.call-update) | async-done | bytes 4194320 | tf_op jit(solution)/shard_map/all_gather | solution.py:49
  85.7 12.0 %fusion.75 = f32[1024,512]{1,0:T(8,128)} fusion(f32[2048,512]{0,1:T(8,128)} %all-gather.4.cloned.1.call-done, f32[1024,2048]{1,0:T(8,128)} %param.7, bf16[1024,2048]{1,0:T(8,128)(2,1)} %param.8), kind=kOutput, calls=%fused_computation.122 | convolution fusion | flops 6446645248 | bytes 18874368 | tf_op jit(solution)/shard_map/dot_general | solution.py:52
  97.7 50.0 %all-reduce.7.cloned.1.call-done = f32[1024,512]{1,0:T(8,128)} async-done(((f32[1024,512]{1,0:T(8,128)}), f32[1024,512]{1,0:T(8,128)}) %all-reduce.7.cloned.1.call-update) | async-done | bytes 2097168 | tf_op jit(solution)/shard_map/psum | solution.py:53
  147.7 6.7 fusion.76
  154.7 78.3 %all-reduce.9.cloned.1.call-done = f32[512,512]{1,0:T(8,128)} async-done(((f32[512,512]{1,0:T(8,128)}), f32[512,512]{1,0:T(8,128)}) %all-reduce.9.cloned.1.call-update) | async-done | bytes 1048592 | tf_op jit(solution)/shard_map/psum | solution.py:54
  233.8 11.7 %custom-call.20 = f32[128,128]{1,0:T(8,128)S(1)} custom-call(f32[128,128]{1,0:T(8,128)S(1)} %slice.125), custom_call_target="Cholesky" | custom-call | tf_op jit(solution)/shard_map/cholesky/custom-call.1 | solution.py:31
  246.9 9.8 %custom-call.21 = f32[1,128,128]{1,2,0:T(8,128)S(1)} custom-call(f32[1,128,128]{2,1,0:T(8,128)S(1)} %fusion.50), custom_call_target="InvertDiagBlocksLowerTriangular" | custom-call | tf_op jit(solution)/shard_map/triangular_solve/custom-call.0 | solution.py:32
  257.0 1.3 fusion.44
  258.2 1.7 convolution_subtract_fusion.3
  259.9 11.7 %custom-call.22 = f32[128,128]{1,0:T(8,128)S(1)} custom-call(f32[128,128]{1,0:T(8,128)S(1)} %slice.130), custom_call_target="Cholesky" | custom-call | tf_op jit(solution)/shard_map/cholesky/custom-call.1 | solution.py:31
  273.0 10.2 %custom-call.23 = f32[1,128,128]{1,2,0:T(8,128)S(1)} custom-call(f32[1,128,128]{2,1,0:T(8,128)S(1)} %fusion.51), custom_call_target="InvertDiagBlocksLowerTriangular" | custom-call | tf_op jit(solution)/shard_map/triangular_solve/custom-call.0 | solution.py:32
  284.2 11.7 %custom-call.24 = f32[128,128]{1,0:T(8,128)S(1)} custom-call(f32[128,128]{1,0:T(8,128)S(1)} %slice.135), custom_call_target="Cholesky" | custom-call | tf_op jit(solution)/shard_map/cholesky/custom-call.1 | solution.py:31
  297.2 9.8 %custom-call.25 = f32[1,128,128]{1,2,0:T(8,128)S(1)} custom-call(f32[1,128,128]{2,1,0:T(8,128)S(1)} %fusion.52), custom_call_target="InvertDiagBlocksLowerTriangular" | custom-call | tf_op jit(solution)/shard_map/triangular_solve/custom-call.0 | solution.py:32
  307.9 11.7 %custom-call.26 = f32[128,128]{1,0:T(8,128)S(1)} custom-call(f32[128,128]{1,0:T(8,128)S(1)} %convolution_subtract_fusion.9), custom_call_target="Cholesky" | custom-call | tf_op jit(solution)/shard_map/cholesky/custom-call.1 | solution.py:31
  320.9 10.0 %custom-call.27 = f32[1,128,128]{1,2,0:T(8,128)S(1)} custom-call(f32[1,128,128]{2,1,0:T(8,128)S(1)} %fusion.53), custom_call_target="InvertDiagBlocksLowerTriangular" | custom-call | tf_op jit(solution)/shard_map/triangular_solve/custom-call.0 | solution.py:32
  331.8 1.9 slice_subtract_fusion.1
  334.4 1.1 convolution_subtract_fusion.1
  337.7 11.1 %fusion.3 = f32[2048,512]{0,1:T(8,128)} fusion(f32[1024,128]{0,1:T(8,128)S(1)} %fusion.77, f32[1024,128]{0,1:T(8,128)S(1)} %fusion.19, f32[1024,128]{0,1:T(8,128)S(1)} %fusion.21, f32[1024,128]{0,1:T(8,128)S(1)} %fusion.23, f32[1024,2048]{1,0:T(8,128)} %param.7, bf16[1024,2048]{1,0:T(8,128)(2,1)S(1)} %copy-done), kind=kOutput, calls=%fused_computation.6 | convolution fusion | flops 6448218112 | bytes 18874368 | tf_op jit(solution)/shard_map/dot_general | solution.py:56
  348.8 88.0 %reduce-scatter.3.cloned.1.call-done = f32[2048,64]{0,1:T(8,128)} async-done(((f32[2048,512]{0,1:T(8,128)}), f32[2048,64]{0,1:T(8,128)}) %reduce-scatter.3.cloned.1.call-update) | async-done | bytes 524304 | tf_op jit(solution)/shard_map/reduce_scatter | solution.py:59
  438.1 1.2 multiply_reduce_fusion.1
  439.3 6.2 psum.44
  445.6 21.6 %all-reduce = f32[512]{0:T(512)S(1)} all-reduce(f32[512]{0:T(512)S(1)} %bitcast_dynamic-update-slice_fusion), channel_id=1, replica_groups=mesh['row'=8,'col'=4] {'row'}, use_global_device_ids=true, to_apply=%add | all-reduce | flops 512 | bytes 4096
  467.2 44.4 %all-gather.6.cloned.1.call-done = f32[2048,512]{0,1:T(8,128)} async-done(((f32[2048,64]{0,1:T(8,128)}), f32[2048,512]{0,1:T(8,128)}) %all-gather.6.cloned.1.call-update) | async-done | bytes 4194320 | tf_op jit(solution)/shard_map/all_gather | solution.py:64
  511.6 12.2 %fusion.1 = f32[1024,512]{1,0:T(8,128)} fusion(f32[2048,512]{0,1:T(8,128)} %all-gather.6.cloned.1.call-done, f32[512]{0:T(512)S(1)} %all-reduce, f32[1024,2048]{1,0:T(8,128)} %param.7, bf16[1024,2048]{1,0:T(8,128)(2,1)} %param.8), kind=kOutput, calls=%fused_computation.4 | convolution fusion | flops 6447693824 | bytes 18876416 | tf_op jit(solution)/shard_map/dot_general | solution.py:52
  523.8 50.0 %all-reduce.11.cloned.1.call-done = f32[1024,512]{1,0:T(8,128)} async-done(((f32[1024,512]{1,0:T(8,128)}), f32[1024,512]{1,0:T(8,128)}) %all-reduce.11.cloned.1.call-update) | async-done | bytes 2097168 | tf_op jit(solution)/shard_map/psum | solution.py:53
  573.8 6.7 fusion.78
  581.0 78.1 %all-reduce.13.cloned.1.call-done = f32[512,512]{1,0:T(8,128)} async-done(((f32[512,512]{1,0:T(8,128)}), f32[512,512]{1,0:T(8,128)}) %all-reduce.13.cloned.1.call-update) | async-done | bytes 1048592 | tf_op jit(solution)/shard_map/psum | solution.py:54
  659.9 11.7 %custom-call.28 = f32[128,128]{1,0:T(8,128)S(1)} custom-call(f32[128,128]{1,0:T(8,128)S(1)} %slice.140), custom_call_target="Cholesky" | custom-call | tf_op jit(solution)/shard_map/cholesky/custom-call.1 | solution.py:31
  672.9 9.8 %custom-call.29 = f32[1,128,128]{1,2,0:T(8,128)S(1)} custom-call(f32[1,128,128]{2,1,0:T(8,128)S(1)} %fusion.54), custom_call_target="InvertDiagBlocksLowerTriangular" | custom-call | tf_op jit(solution)/shard_map/triangular_solve/custom-call.0 | solution.py:32
  683.1 1.3 fusion.42
  684.3 1.7 convolution_subtract_fusion.2
  686.1 11.7 %custom-call.30 = f32[128,128]{1,0:T(8,128)S(1)} custom-call(f32[128,128]{1,0:T(8,128)S(1)} %slice.145), custom_call_target="Cholesky" | custom-call | tf_op jit(solution)/shard_map/cholesky/custom-call.1 | solution.py:31
  699.1 10.0 %custom-call.31 = f32[1,128,128]{1,2,0:T(8,128)S(1)} custom-call(f32[1,128,128]{2,1,0:T(8,128)S(1)} %fusion.55), custom_call_target="InvertDiagBlocksLowerTriangular" | custom-call | tf_op jit(solution)/shard_map/triangular_solve/custom-call.0 | solution.py:32
  710.7 11.7 %custom-call.32 = f32[128,128]{1,0:T(8,128)S(1)} custom-call(f32[128,128]{1,0:T(8,128)S(1)} %slice.150), custom_call_target="Cholesky" | custom-call | tf_op jit(solution)/shard_map/cholesky/custom-call.1 | solution.py:31
  723.7 9.8 %custom-call.33 = f32[1,128,128]{1,2,0:T(8,128)S(1)} custom-call(f32[1,128,128]{2,1,0:T(8,128)S(1)} %fusion.56), custom_call_target="InvertDiagBlocksLowerTriangular" | custom-call | tf_op jit(solution)/shard_map/triangular_solve/custom-call.0 | solution.py:32
  734.4 11.7 %custom-call.34 = f32[128,128]{1,0:T(8,128)S(1)} custom-call(f32[128,128]{1,0:T(8,128)S(1)} %convolution_subtract_fusion.8), custom_call_target="Cholesky" | custom-call | tf_op jit(solution)/shard_map/cholesky/custom-call.1 | solution.py:31
  747.6 9.8 %custom-call.35 = f32[1,128,128]{1,2,0:T(8,128)S(1)} custom-call(f32[1,128,128]{2,1,0:T(8,128)S(1)} %fusion.57), custom_call_target="InvertDiagBlocksLowerTriangular" | custom-call | tf_op jit(solution)/shard_map/triangular_solve/custom-call.0 | solution.py:32
  757.7 1.4 fusion.17
  759.2 1.9 slice_subtract_fusion
  765.0 10.9 %fusion.25 = f32[2048,512]{0,1:T(8,128)} fusion(f32[1024,128]{0,1:T(8,128)S(1)} %fusion.79, f32[1024,128]{0,1:T(8,128)S(1)} %fusion.13, f32[1024,128]{0,1:T(8,128)S(1)} %fusion.15, f32[1024,128]{0,1:T(8,128)S(1)} %fusion.17, f32[1024,2048]{1,0:T(8,128)} %param.7, bf16[1024,2048]{1,0:T(8,128)(2,1)S(1)} %copy-done.1), kind=kOutput, calls=%fused_computation.43 | convolution fusion | flops 6448218112 | bytes 18874368 | tf_op jit(solution)/shard_map/dot_general | solution.py:56
  776.0 88.0 %reduce-scatter.5.cloned.1.call-done = f32[2048,64]{0,1:T(8,128)} async-done(((f32[2048,512]{0,1:T(8,128)}), f32[2048,64]{0,1:T(8,128)}) %reduce-scatter.5.cloned.1.call-update) | async-done | bytes 524304 | tf_op jit(solution)/shard_map/reduce_scatter | solution.py:59
  864.0 1.2 multiply_reduce_fusion
  865.2 6.2 psum.47
  871.5 21.6 %all-reduce.1 = f32[512]{0:T(512)S(1)} all-reduce(f32[512]{0:T(512)S(1)} %fusion.74), channel_id=1, replica_groups=mesh['row'=8,'col'=4] {'row'}, use_global_device_ids=true, to_apply=%add.1 | all-reduce | flops 512 | bytes 4096
  893.1 1.9 broadcast_divide_fusion
  895.0 43.9 %all-gather.8.cloned.1.call-done = f32[2048,512]{0,1:T(8,128)} async-done(((f32[2048,64]{0,1:T(8,128)}), f32[2048,512]{0,1:T(8,128)}) %all-gather.8.cloned.1.call-update) | async-done | bytes 4194320 | tf_op jit(solution)/shard_map/all_gather | solution.py:64
  938.9 13.9 %multiply_subtract_fusion = f32[1024,2048]{1,0:T(8,128)} fusion(f32[2048,512]{0,1:T(8,128)} %all-gather.8.cloned.1.call-done, f32[1024,128]{0,1:T(8,128)S(1)} %fusion.79, f32[1024,128]{0,1:T(8,128)S(1)} %fusion.13, f32[1024,128]{0,1:T(8,128)S(1)} %fusion.15, f32[1024,128]{0,1:T(8,128)S(1)} %fusion.17, f32[1024,2048]{1,0:T(8,128)} %param.7, ...), kind=kOutput, calls=%fused_computation.1 | convolution fusion | flops 6452412416 | bytes 27262976 | tf_op jit(solution)/shard_map/dot_general | solution.py:69
  952.8 9.3 subtract_convert_fusion
  (100 shorter events, 27.6 us)
Async XLA Ops:
  7.2 78.5 %all-gather.4.cloned.1.call-start = ((), (), s32[]{:S(2)}) async-start(), calls=%async_computation.2 | async-start | bytes 4718592 | tf_op jit(solution)/shard_map/all_gather | solution.py:49
  7.9 139.8 %all-reduce.7.cloned.1.call-start = ((), (), s32[]{:S(2)}) async-start(), calls=%async_computation.3 | async-start | bytes 4194304 | tf_op jit(solution)/shard_map/psum | solution.py:53
  97.7 135.3 %all-reduce.9.cloned.1.call-start = ((), (), s32[]{:S(2)}) async-start(), calls=%async_computation.4 | async-start | bytes 2097152 | tf_op jit(solution)/shard_map/psum | solution.py:54
  154.4 176.8 %copy-start.2 = (f32[1024,512]{1,0:T(8,128)S(1)}, f32[1024,512]{1,0:T(8,128)}, u32[]{:S(2)}) copy-start(f32[1024,512]{1,0:T(8,128)} %all-reduce.7.cloned.1.call-done) | copy-start | bytes 6291460
  154.4 282.4 %reduce-scatter.3.cloned.1.call-start = ((), (), s32[]{:S(2)}) async-start(), calls=%async_computation.5 | async-start | bytes 4718592 | tf_op jit(solution)/shard_map/reduce_scatter | solution.py:59
  333.7 3.9 copy-start
  348.7 88.2 %copy-start.9 = (u32[32]{0:T(128)S(1)}, u32[32]{0:T(128)}, u32[]{:S(2)}) copy-start(u32[32]{0:T(128)} %constant.27) | copy-start | bytes 388
  348.8 162.8 %all-gather.6.cloned.1.call-start = ((), (), s32[]{:S(2)}) async-start(), calls=%async_computation.6 | async-start | bytes 4718592 | tf_op jit(solution)/shard_map/all_gather | solution.py:64
  436.8 137.0 %all-reduce.11.cloned.1.call-start = ((), (), s32[]{:S(2)}) async-start(), calls=%async_computation.7 | async-start | bytes 4194304 | tf_op jit(solution)/shard_map/psum | solution.py:53
  523.8 135.3 %all-reduce.13.cloned.1.call-start = ((), (), s32[]{:S(2)}) async-start(), calls=%async_computation.8 | async-start | bytes 2097152 | tf_op jit(solution)/shard_map/psum | solution.py:54
  580.5 177.2 %copy-start.3 = (f32[1024,512]{1,0:T(8,128)S(1)}, f32[1024,512]{1,0:T(8,128)}, u32[]{:S(2)}) copy-start(f32[1024,512]{1,0:T(8,128)} %all-reduce.11.cloned.1.call-done) | copy-start | bytes 6291460
  580.5 283.5 %reduce-scatter.5.cloned.1.call-start = ((), (), s32[]{:S(2)}) async-start(), calls=%async_computation.9 | async-start | bytes 4718592 | tf_op jit(solution)/shard_map/reduce_scatter | solution.py:59
  683.0 26.3 %copy-start.5 = (f32[128,128]{1,0:T(8,128)}, f32[128,128]{1,0:T(8,128)S(1)}, u32[]{:S(2)}) copy-start(f32[128,128]{1,0:T(8,128)S(1)} %fusion.32) | copy-start | bytes 196612
  709.4 0.6 copy-start.6
  710.7 50.4 %copy-start.7 = (f32[128,128]{1,0:T(8,128)S(1)}, f32[128,128]{1,0:T(8,128)}, u32[]{:S(2)}) copy-start(f32[128,128]{1,0:T(8,128)} %copy-done.6) | copy-start | bytes 196612
  761.1 3.9 copy-start.1
  775.9 162.9 %all-gather.8.cloned.1.call-start = ((), (), s32[]{:S(2)}) async-start(), calls=%async_computation.10 | async-start | bytes 4718592 | tf_op jit(solution)/shard_map/all_gather | solution.py:64
  938.9 13.9 %copy-start.4 = (f32[2048,512]{0,1:T(8,128)S(1)}, f32[2048,512]{0,1:T(8,128)}, u32[]{:S(2)}) copy-start(f32[2048,512]{0,1:T(8,128)} %all-gather.8.cloned.1.call-done) | copy-start | bytes 12582916
  938.9 13.9 %copy-start.8 = (bf16[1024,2048]{1,0:T(8,128)(2,1)S(1)}, bf16[1024,2048]{1,0:T(8,128)(2,1)}, u32[]{:S(2)}) copy-start(bf16[1024,2048]{1,0:T(8,128)(2,1)} %param.9) | copy-start | bytes 12582916
Sparse Core Ops, SparseCore 0:
  10.1 75.5 all-gather.3
  97.8 49.9 all-reduce.6
  154.5 78.3 all-reduce.8
  348.9 87.8 reduce-scatter.2
  438.8 72.7 all-gather.5
  523.9 49.8 all-reduce.10
  580.6 78.3 all-reduce.12
  776.0 87.8 reduce-scatter.4
  866.1 72.6 all-gather.7
where the time goes:
time: 975 us; the launch traced here: 969 us
  waiting for transfers between devices  599 us (61%)
  other arithmetic  188 us (19%)
  matrix products  107 us (11%)
  blocking collectives  55.5 us (6%)
  between operations  15.6 us (2%)
    reduce_scatter x2, waiting for transfers between devices, shards(): lax.psum_scatter(transposed, 'row', scatter_dimension=1, tiled=True)  176 us
    psum x2, waiting for transfers between devices, shards(): gram_sum = lax.psum(self_gram(left_sum), 'row')  156 us
    psum x2, waiting for transfers between devices, shards(): left_sum = lax.psum(partials, 'col')  100 us
    another operation x24, other arithmetic, solve_rows(): corner = lax.linalg.cholesky(trailing[:size, :size], symmetrize_input=False)  99.1 us
    all_gather x2, waiting for transfers between devices, shards(): lax.all_gather(products, 'row', axis=1, tiled=True)  88.2 us
    another operation x16, other arithmetic, solve_rows(): lax.linalg.triangular_solve(corner, jnp.eye(size, dtype=corner.dtype), le...  84.4 us
    all_gather x1, waiting for transfers between devices, shards(): right_full = lax.all_gather(right_start, 'row', axis=1, tiled=True)  77.7 us
    unnamed x2, blocking collectives  43.1 us
  transfers between devices with their start and end apart: 9, of which 9 were waited for; matrix products, arithmetic and copies ran while one was open for 1% of the time, Pallas kernels for 0%

commit v1 on v0

--- a/solution.py
+++ b/solution.py
@@ -51,7 +51,9 @@
     for iteration in range(ITERS):
         partials = jnp.dot(blended, right_full, precision=wide_mode)
         left_sum = lax.psum(partials, "col")
-        gram_sum = lax.psum(self_gram(left_sum), "row")
+        x = self_gram(left_sum)
+        shards_2 = lax.all_gather(x, "row", axis=0, tiled=False)
+        gram_sum = shards_2.sum(axis=0)
         left_rows = solve_rows(left_sum, gram_sum)
         transposed = lax.dot_general(
             blended, left_rows, (((0,), (0,)), ((), ())), precision=wide_mode

time: 975 us -> 1070 us (1.097)
  waiting for transfers between devices: 599 us -> 689 us
    all_gather x0 -> x2, waiting for transfers between devices: none -> 249 us  [shards(): shards_2 = lax.all_gather(x, 'row', axis=0, tiled=False)]
    psum x2 -> x0, waiting for transfers between devices: 156 us -> none  [shards(): gram_sum = lax.psum(self_gram(left_sum), 'row')]
  transfers between devices with their start and end apart: 9 -> 9, of which waited for: 9 -> 9; matrix products, arithmetic and copies ran while one was open for 1% -> 0% of each run, Pallas kernels for 0% -> 0%
where the time goes in v1:
time: 1070 us
  waiting for transfers between devices  689 us (64%)
  other arithmetic  197 us (18%)
  matrix products  106 us (10%)
  blocking collectives  55.5 us (5%)
  between operations  15.4 us (1%)
    all_gather x2, waiting for transfers between devices, shards(): shards_2 = lax.all_gather(x, 'row', axis=0, tiled=False)  249 us
    reduce_scatter x2, waiting for transfers between devices, shards(): lax.psum_scatter(transposed, 'row', scatter_dimension=1, tiled=True)  173 us
    psum x2, waiting for transfers between devices, shards(): left_sum = lax.psum(partials, 'col')  100 us
    another operation x24, other arithmetic, solve_rows(): corner = lax.linalg.cholesky(trailing[:size, :size], symmetrize_input=False)  99.5 us
    all_gather x2, waiting for transfers between devices, shards(): lax.all_gather(products, 'row', axis=1, tiled=True)  88.2 us
    another operation x16, other arithmetic, solve_rows(): lax.linalg.triangular_solve(corner, jnp.eye(size, dtype=corner.dtype), le...  84.3 us
    all_gather x1, waiting for transfers between devices, shards(): right_full = lax.all_gather(right_start, 'row', axis=1, tiled=True)  77.7 us
    unnamed x2, blocking collectives  43.2 us
  transfers between devices with their start and end apart: 9, of which 9 were waited for; matrix products, arithmetic and copies ran while one was open for 0% of the time, Pallas kernels for 0%

profile of v1, /device:TPU:0, one launch (start us, length us, event | category | flops | bytes accessed | tf_op | source)
XLA Modules:
  0.0 1066.0 jit_solution(6857507136681068155)
XLA Ops:
  7.9 77.7 %all-gather.8.cloned.1.call-done = f32[2048,512]{0,1:T(8,128)} async-done(((f32[2048,64]{0,1:T(8,128)}), f32[2048,512]{0,1:T(8,128)}) %all-gather.8.cloned.1.call-update) | async-done | bytes 4194320 | tf_op jit(solution)/shard_map/all_gather | solution.py:49
  85.7 12.0 %fusion.75 = f32[1024,512]{1,0:T(8,128)} fusion(f32[2048,512]{0,1:T(8,128)} %all-gather.8.cloned.1.call-done, f32[1024,2048]{1,0:T(8,128)} %param.7, bf16[1024,2048]{1,0:T(8,128)(2,1)} %param.8), kind=kOutput, calls=%fused_computation.122 | convolution fusion | flops 6446645248 | bytes 18874368 | tf_op jit(solution)/shard_map/dot_general | solution.py:52
  97.7 50.0 %all-reduce.5.cloned.1.call-done = f32[1024,512]{1,0:T(8,128)} async-done(((f32[1024,512]{1,0:T(8,128)}), f32[1024,512]{1,0:T(8,128)}) %all-reduce.5.cloned.1.call-update) | async-done | bytes 2097168 | tf_op jit(solution)/shard_map/psum | solution.py:53
  147.7 6.7 fusion.76
  154.7 124.5 %all-gather.14.cloned.1.call-done = f32[4096,512]{1,0:T(8,128)} async-done(((f32[512,512]{1,0:T(8,128)}), f32[4096,512]{1,0:T(8,128)}) %all-gather.14.cloned.1.call-update) | async-done | bytes 8388624 | tf_op jit(solution)/shard_map/all_gather | solution.py:55
  279.2 4.5 reduce_sum.36
  283.7 11.7 %custom-call.20 = f32[128,128]{1,0:T(8,128)S(1)} custom-call(f32[128,128]{1,0:T(8,128)S(1)} %slice.125), custom_call_target="Cholesky" | custom-call | tf_op jit(solution)/shard_map/cholesky/custom-call.1 | solution.py:31
  296.8 9.8 custom-call.21
  308.7 11.7 %custom-call.22 = f32[128,128]{1,0:T(8,128)S(1)} custom-call(f32[128,128]{1,0:T(8,128)S(1)} %slice.130), custom_call_target="Cholesky" | custom-call | tf_op jit(solution)/shard_map/cholesky/custom-call.1 | solution.py:31
  322.1 9.8 custom-call.23
  332.2 1.2 fusion.48
  333.4 1.3 convolution_subtract_fusion.7
  334.8 11.7 %custom-call.24 = f32[128,128]{1,0:T(8,128)S(1)} custom-call(f32[128,128]{1,0:T(8,128)S(1)} %slice.135), custom_call_target="Cholesky" | custom-call | tf_op jit(solution)/shard_map/cholesky/custom-call.1 | solution.py:31
  347.8 9.8 custom-call.25
  358.5 11.9 %custom-call.26 = f32[128,128]{1,0:T(8,128)S(1)} custom-call(f32[128,128]{1,0:T(8,128)S(1)} %convolution_subtract_fusion.9), custom_call_target="Cholesky" | custom-call | tf_op jit(solution)/shard_map/cholesky/custom-call.1 | solution.py:31
  371.7 9.8 custom-call.27
  382.4 1.9 slice_subtract_fusion.1
  388.3 11.1 %fusion.3 = f32[2048,512]{0,1:T(8,128)} fusion(f32[1024,128]{0,1:T(8,128)S(1)} %fusion.77, f32[1024,128]{0,1:T(8,128)S(1)} %fusion.19, f32[1024,128]{0,1:T(8,128)S(1)} %fusion.21, f32[1024,128]{0,1:T(8,128)S(1)} %fusion.23, f32[1024,2048]{1,0:T(8,128)} %param.7, bf16[1024,2048]{1,0:T(8,128)(2,1)S(1)} %copy-done), kind=kOutput, calls=%fused_computation.6 | convolution fusion | flops 6448218112 | bytes 18874368 | tf_op jit(solution)/shard_map/dot_general | solution.py:58
  399.4 86.6 %reduce-scatter.3.cloned.1.call-done = f32[2048,64]{0,1:T(8,128)} async-done(((f32[2048,512]{0,1:T(8,128)}), f32[2048,64]{0,1:T(8,128)}) %reduce-scatter.3.cloned.1.call-update) | async-done | bytes 524304 | tf_op jit(solution)/shard_map/reduce_scatter | solution.py:61
  487.3 1.2 multiply_reduce_fusion.1
  488.5 6.2 psum.29
  494.8 21.6 %all-reduce = f32[512]{0:T(512)S(1)} all-reduce(f32[512]{0:T(512)S(1)} %bitcast_dynamic-update-slice_fusion), channel_id=1, replica_groups=mesh['row'=8,'col'=4] {'row'}, use_global_device_ids=true, to_apply=%add | all-reduce | flops 512 | bytes 4096
  516.4 44.4 %all-gather.10.cloned.1.call-done = f32[2048,512]{0,1:T(8,128)} async-done(((f32[2048,64]{0,1:T(8,128)}), f32[2048,512]{0,1:T(8,128)}) %all-gather.10.cloned.1.call-update) | async-done | bytes 4194320 | tf_op jit(solution)/shard_map/all_gather | solution.py:66
  560.7 12.2 %fusion.1 = f32[1024,512]{1,0:T(8,128)} fusion(f32[2048,512]{0,1:T(8,128)} %all-gather.10.cloned.1.call-done, f32[512]{0:T(512)S(1)} %all-reduce, f32[1024,2048]{1,0:T(8,128)} %param.7, bf16[1024,2048]{1,0:T(8,128)(2,1)} %param.8), kind=kOutput, calls=%fused_computation.4 | convolution fusion | flops 6447693824 | bytes 18876416 | tf_op jit(solution)/shard_map/dot_general | solution.py:52
  573.0 50.0 %all-reduce.7.cloned.1.call-done = f32[1024,512]{1,0:T(8,128)} async-done(((f32[1024,512]{1,0:T(8,128)}), f32[1024,512]{1,0:T(8,128)}) %all-reduce.7.cloned.1.call-update) | async-done | bytes 2097168 | tf_op jit(solution)/shard_map/psum | solution.py:53
  623.0 6.7 fusion.78
  630.2 124.3 %all-gather.16.cloned.1.call-done = f32[4096,512]{1,0:T(8,128)} async-done(((f32[512,512]{1,0:T(8,128)}), f32[4096,512]{1,0:T(8,128)}) %all-gather.16.cloned.1.call-update) | async-done | bytes 8388624 | tf_op jit(solution)/shard_map/all_gather | solution.py:55
  754.5 4.5 reduce_sum.38
  759.0 11.7 %custom-call.28 = f32[128,128]{1,0:T(8,128)S(1)} custom-call(f32[128,128]{1,0:T(8,128)S(1)} %slice.140), custom_call_target="Cholesky" | custom-call | tf_op jit(solution)/shard_map/cholesky/custom-call.1 | solution.py:31
  772.0 9.8 custom-call.29
  784.0 11.7 %custom-call.30 = f32[128,128]{1,0:T(8,128)S(1)} custom-call(f32[128,128]{1,0:T(8,128)S(1)} %slice.145), custom_call_target="Cholesky" | custom-call | tf_op jit(solution)/shard_map/cholesky/custom-call.1 | solution.py:31
  797.2 9.8 custom-call.31
  807.3 1.2 fusion.46
  808.5 1.3 convolution_subtract_fusion.6
  809.8 11.7 %custom-call.32 = f32[128,128]{1,0:T(8,128)S(1)} custom-call(f32[128,128]{1,0:T(8,128)S(1)} %slice.150), custom_call_target="Cholesky" | custom-call | tf_op jit(solution)/shard_map/cholesky/custom-call.1 | solution.py:31
  822.9 9.8 custom-call.33
  833.5 11.9 %custom-call.34 = f32[128,128]{1,0:T(8,128)S(1)} custom-call(f32[128,128]{1,0:T(8,128)S(1)} %convolution_subtract_fusion.8), custom_call_target="Cholesky" | custom-call | tf_op jit(solution)/shard_map/cholesky/custom-call.1 | solution.py:31
  846.8 9.8 custom-call.35
  857.5 1.9 slice_subtract_fusion
  863.3 10.9 %fusion.25 = f32[2048,512]{0,1:T(8,128)} fusion(f32[1024,128]{0,1:T(8,128)S(1)} %fusion.79, f32[1024,128]{0,1:T(8,128)S(1)} %fusion.13, f32[1024,128]{0,1:T(8,128)S(1)} %fusion.15, f32[1024,128]{0,1:T(8,128)S(1)} %fusion.17, f32[1024,2048]{1,0:T(8,128)} %param.7, bf16[1024,2048]{1,0:T(8,128)(2,1)S(1)} %copy-done.1), kind=kOutput, calls=%fused_computation.43 | convolution fusion | flops 6448218112 | bytes 18874368 | tf_op jit(solution)/shard_map/dot_general | solution.py:58
  874.3 86.6 %reduce-scatter.5.cloned.1.call-done = f32[2048,64]{0,1:T(8,128)} async-done(((f32[2048,512]{0,1:T(8,128)}), f32[2048,64]{0,1:T(8,128)}) %reduce-scatter.5.cloned.1.call-update) | async-done | bytes 524304 | tf_op jit(solution)/shard_map/reduce_scatter | solution.py:61
  960.9 1.2 multiply_reduce_fusion
  962.1 6.2 psum.31
  968.4 21.6 %all-reduce.1 = f32[512]{0:T(512)S(1)} all-reduce(f32[512]{0:T(512)S(1)} %fusion.74), channel_id=1, replica_groups=mesh['row'=8,'col'=4] {'row'}, use_global_device_ids=true, to_apply=%add.1 | all-reduce | flops 512 | bytes 4096
  990.0 1.9 broadcast_divide_fusion
  991.9 43.8 %all-gather.12.cloned.1.call-done = f32[2048,512]{0,1:T(8,128)} async-done(((f32[2048,64]{0,1:T(8,128)}), f32[2048,512]{0,1:T(8,128)}) %all-gather.12.cloned.1.call-update) | async-done | bytes 4194320 | tf_op jit(solution)/shard_map/all_gather | solution.py:66
  1035.8 13.9 %multiply_subtract_fusion = f32[1024,2048]{1,0:T(8,128)} fusion(f32[2048,512]{0,1:T(8,128)} %all-gather.12.cloned.1.call-done, f32[1024,128]{0,1:T(8,128)S(1)} %fusion.79, f32[1024,128]{0,1:T(8,128)S(1)} %fusion.13, f32[1024,128]{0,1:T(8,128)S(1)} %fusion.15, f32[1024,128]{0,1:T(8,128)S(1)} %fusion.17, f32[1024,2048]{1,0:T(8,128)} %param.7, ...), kind=kOutput, calls=%fused_computation.1 | convolution fusion | flops 6452412416 | bytes 27262976 | tf_op jit(solution)/shard_map/dot_general | solution.py:71
  1049.7 9.3 subtract_convert_fusion
  (100 shorter events, 29.7 us)
Async XLA Ops:
  7.2 78.5 %all-gather.8.cloned.1.call-start = ((), (), s32[]{:S(2)}) async-start(), calls=%async_computation.2 | async-start | bytes 4718592 | tf_op jit(solution)/shard_map/all_gather | solution.py:49
  7.9 139.8 %all-reduce.5.cloned.1.call-start = ((), (), s32[]{:S(2)}) async-start(), calls=%async_computation.3 | async-start | bytes 4194304 | tf_op jit(solution)/shard_map/psum | solution.py:53
  97.7 181.5 %all-gather.14.cloned.1.call-start = ((), (), s32[]{:S(2)}) async-start(), calls=%async_computation.9 | async-start | bytes 9437184 | tf_op jit(solution)/shard_map/all_gather | solution.py:55
  154.5 331.5 %reduce-scatter.3.cloned.1.call-start = ((), (), s32[]{:S(2)}) async-start(), calls=%async_computation.4 | async-start | bytes 4718592 | tf_op jit(solution)/shard_map/reduce_scatter | solution.py:61
  283.7 98.1 %copy-start.2 = (f32[1024,512]{1,0:T(8,128)S(1)}, f32[1024,512]{1,0:T(8,128)}, u32[]{:S(2)}) copy-start(f32[1024,512]{1,0:T(8,128)} %all-reduce.5.cloned.1.call-done) | copy-start | bytes 6291460
  307.9 0.8 copy-start.5
  384.3 3.9 copy-start
  399.3 86.8 %copy-start.8 = (u32[32]{0:T(128)S(1)}, u32[32]{0:T(128)}, u32[]{:S(2)}) copy-start(u32[32]{0:T(128)} %constant.27) | copy-start | bytes 388
  399.3 161.4 %all-gather.10.cloned.1.call-start = ((), (), s32[]{:S(2)}) async-start(), calls=%async_computation.5 | async-start | bytes 4718592 | tf_op jit(solution)/shard_map/all_gather | solution.py:66
  486.0 137.0 %all-reduce.7.cloned.1.call-start = ((), (), s32[]{:S(2)}) async-start(), calls=%async_computation.6 | async-start | bytes 4194304 | tf_op jit(solution)/shard_map/psum | solution.py:53
  572.9 181.5 %all-gather.16.cloned.1.call-start = ((), (), s32[]{:S(2)}) async-start(), calls=%async_computation.10 | async-start | bytes 9437184 | tf_op jit(solution)/shard_map/all_gather | solution.py:55
  629.8 331.1 %reduce-scatter.5.cloned.1.call-start = ((), (), s32[]{:S(2)}) async-start(), calls=%async_computation.7 | async-start | bytes 4718592 | tf_op jit(solution)/shard_map/reduce_scatter | solution.py:61
  759.0 97.9 %copy-start.3 = (f32[1024,512]{1,0:T(8,128)S(1)}, f32[1024,512]{1,0:T(8,128)}, u32[]{:S(2)}) copy-start(f32[1024,512]{1,0:T(8,128)} %all-reduce.7.cloned.1.call-done) | copy-start | bytes 6291460
  783.1 0.8 copy-start.6
  859.4 3.9 copy-start.1
  874.2 161.5 %all-gather.12.cloned.1.call-start = ((), (), s32[]{:S(2)}) async-start(), calls=%async_computation.8 | async-start | bytes 4718592 | tf_op jit(solution)/shard_map/all_gather | solution.py:66
  1035.8 13.9 %copy-start.4 = (f32[2048,512]{0,1:T(8,128)S(1)}, f32[2048,512]{0,1:T(8,128)}, u32[]{:S(2)}) copy-start(f32[2048,512]{0,1:T(8,128)} %all-gather.12.cloned.1.call-done) | copy-start | bytes 12582916
  1035.8 13.9 %copy-start.7 = (bf16[1024,2048]{1,0:T(8,128)(2,1)S(1)}, bf16[1024,2048]{1,0:T(8,128)(2,1)}, u32[]{:S(2)}) copy-start(bf16[1024,2048]{1,0:T(8,128)(2,1)} %param.9) | copy-start | bytes 12582916
Sparse Core Ops, SparseCore 0:
  10.1 75.5 all-gather.7
  97.8 49.9 all-reduce.4
  154.6 124.5 all-gather.13
  399.5 86.4 reduce-scatter.2
  488.0 72.7 all-gather.9
  573.1 49.8 all-reduce.6
  629.9 124.5 all-gather.15
  874.4 86.4 reduce-scatter.4
  963.0 72.7 all-gather.11
